TPU v7x, 256 devices: a whole 4x4x8 slice. The times are simulated.
256 devices in a mesh: row: 8 (over y, z_hi), col: 32 (over z_lo, x, core).
Axes of the slice: x: 4, y: 4, z: 8 (z_hi: 2, z_lo: 4; z = z_hi * 4 + z_lo), core: 2. Of those that a mesh axis runs over, the one named last changes fastest.
Arguments:
- transfer: bfloat16 [2, 4096, 16384], P(None, 'row', 'col'), may hold values from -0.046875 to 0.046875
- phase: float32 [16384, 128], P('col', 'row'), may hold values from -3.140625 to 3.140625
- trap_index: int32 [128, 64], replicated, may hold values from 0 to 4095
- levels: int32 [128, 64], replicated, may hold values from 1 to 4
- weights_old: float32 [128, 64], replicated, may hold values from 0.5 to 1.5
Outputs:
- far_field: bfloat16 [4096, 2, 128], P(('row', 'col'))
- weights_new: float32 [128, 64], replicated
- slm_field: float32 [16384, 2, 128], P('col', None, 'row')
All inputs are finite; a program needn't handle non-finite values.
Results may differ from a plain program's by a relative error of at most 0.013.
Values may be sent and summed in bfloat16 or wider, within the bound.
A program may use at most 64 MiB of HBM per device.

v0:
```python
import jax
import jax.numpy as jnp
from jax import lax
from jax.sharding import PartitionSpec as P

MODES = 16384
TRAPS = 64


def back_terms(transfer, piece):
    count = piece.shape[2]
    real_rows = transfer[0]
    imag_rows = transfer[1]
    stacked = jnp.concatenate([piece[:, 0], piece[:, 1]], axis=1)
    dims = (((0,), (0,)), ((), ()))
    first_b = lax.dot_general(real_rows, stacked, dims, preferred_element_type=jnp.float32)
    second_b = lax.dot_general(imag_rows, stacked, dims, preferred_element_type=jnp.float32)
    part = jnp.concatenate(
        [first_b[:, :count] + second_b[:, count:], first_b[:, count:] - second_b[:, :count]], axis=1
    )
    return part


def trap_lookup(block, trap_index, offset):
    count = block.shape[2]
    height = block.shape[0]
    local = trap_index - offset
    inside = (local >= 0) & (local < height)
    clipped = jnp.clip(local, 0, height - 1)
    pattern_ids = jnp.arange(count, dtype=jnp.int32)[:, None]
    values = block[clipped, :, pattern_ids]
    return (inside, clipped, pattern_ids, values)


def body(transfer, phase, trap_index, levels, weights_old):
    n_col = lax.axis_size("col")
    tile_rows = transfer.shape[1]
    pix_rows = tile_rows // n_col
    modes_local = transfer.shape[2]
    field = jnp.stack([jnp.cos(phase), jnp.sin(phase)], axis=0).astype(jnp.bfloat16)
    whole = lax.all_gather(field, "row", axis=2, tiled=True)
    count = whole.shape[2]
    joined = jnp.concatenate([whole[0], whole[1]], axis=1)
    target = levels.astype(jnp.float32)
    row_start = lax.axis_index("row") * tile_rows
    real_rows = transfer[0]
    imag_rows = transfer[1]
    first = jnp.dot(real_rows, joined, preferred_element_type=jnp.float32)
    second = jnp.dot(imag_rows, joined, preferred_element_type=jnp.float32)
    mine = lax.psum_scatter(
        jnp.stack(
            [first[:, :count] - second[:, count:], first[:, count:] + second[:, :count]], axis=1
        ),
        "col",
        scatter_dimension=0,
        tiled=True,
    )
    far_field = mine.astype(jnp.bfloat16)
    offset = row_start + lax.axis_index("col") * pix_rows
    inside, clipped, pattern_ids, values = trap_lookup(mine, trap_index, offset)
    amp_local = jnp.sqrt(values[..., 0] ** 2 + values[..., 1] ** 2 + 0.25)
    amp = lax.psum(jnp.where(inside, amp_local, 0.0), ("row", "col"))
    ratio = amp / target
    weights_new = weights_old * jnp.mean(ratio, axis=1, keepdims=True) / ratio
    coef = weights_new * target / amp
    adds = jnp.where(inside[..., None], coef[..., None] * values, 0.0)
    projected = (
        jnp.zeros(mine.shape, jnp.float32)
        .at[clipped, :, pattern_ids]
        .add(adds)
        .astype(jnp.bfloat16)
    )
    total = back_terms(transfer, lax.all_gather(projected, "col", axis=0, tiled=True))
    back = total.reshape(modes_local, 2, count)
    back = lax.psum_scatter(
        back.astype(jnp.bfloat16), "row", scatter_dimension=2, tiled=True
    ).astype(jnp.float32)
    scaled = jnp.sqrt(jnp.float32(MODES) / jnp.float32(TRAPS)) * back
    slm_field = scaled / jnp.sqrt(scaled[:, 0:1] ** 2 + scaled[:, 1:2] ** 2 + 1.0)
    return (far_field, weights_new, slm_field)


def solution(mesh):
    placed = (P(None, "row", "col"), P("col", "row"), P(), P(), P())
    return jax.shard_map(
        body,
        mesh=mesh,
        in_specs=placed,
        out_specs=(P(("row", "col"), None, None), P(), P("col", None, "row")),
        check_vma=False,
    )
```

profile of v0, /device:TPU:2, one launch (start us, length us, event | category | flops | bytes accessed | tf_op | source)
XLA Modules:
  0.0 716.5 jit_solution(8957432366630390848)
XLA Ops:
  7.2 0.9 fusion.20
  8.2 46.2 %all_gather.6 = bf16[2,512,128]{1,2,0:T(8,128)(2,1)S(1)} all-gather(bf16[2,512,16]{1,2,0:T(8,128)(2,1)S(1)} %pad_maximum_fusion.8), channel_id=1, replica_groups=mesh['row'=8,'col'=32] {'row'}, dimensions={2}, use_global_device_ids=true | all-gather | bytes 294912 | tf_op jit(solution)/shard_map/all_gather | solution.py:41
  54.3 1.4 convolution_bitcast_fusion.2
  55.7 1.4 convolution_bitcast_fusion.3
  57.1 0.1 fusion.13
  57.2 1.0 copy.31
  58.4 0.1 and_reduce_fusion
  58.5 0.1 copy.36
  58.7 0.1 copy.32
  58.9 0.6 dynamic-slice
  60.1 273.9 %all-reduce.3.cloned.1.call-done = f32[512,2,128]{2,1,0:T(2,128)} async-done(((f32[512,2,128]{2,1,0:T(2,128)}), f32[512,2,128]{2,1,0:T(2,128)}) %all-reduce.3.cloned.1.call-update) | async-done | bytes 524304
  334.0 1.3 fusion.27
  335.3 0.4 copy.33
  335.7 88.8 %gather_fusion = f32[8192,2]{1,0:T(8,128)} fusion(f32[16,2,128]{1,2,0:T(8,128)S(1)} %copy.33, s32[8192]{0:T(1024)S(1)} %reshape.27), kind=kCustom, calls=%fused_computation | custom fusion | bytes 196608 | tf_op jit(solution)/shard_map/gather | solution.py:31
  424.5 8.0 %fusion.28 = (f32[128,64,1]{2,1,0:T(8,128)}, f32[128,64,1]{2,1,0:T(8,128)}) fusion(f32[128,64,2]{2,1,0:T(8,128)} %bitcast.49), kind=kLoop, calls=%fused_computation.66 | loop fusion | bytes 131072 | tf_op jit(solution)/shard_map/slice | solution.py:61
  432.5 3.8 copy.40
  436.3 3.7 copy.41
  440.0 81.6 %psum.7 = f32[128,64]{0,1:T(8,128)S(1)} all-reduce(f32[128,64]{0,1:T(8,128)S(1)} %get-tuple-element.14), channel_id=1, replica_groups=mesh['row'=8,'col'=32] {'row','col'}, use_global_device_ids=true, to_apply=%region_1.2 | all-reduce | flops 8192 | bytes 65536 | tf_op jit(solution)/shard_map/psum | solution.py:62
  521.7 0.1 copy.37
  521.8 0.6 multiply_divide_fusion
  522.5 0.1 copy.38
  522.6 7.7 %multiply_select_fusion = f32[128,64,2]{2,1,0:T(8,128)} fusion(f32[128,64,2]{2,1,0:T(8,128)} %bitcast.50, f32[128,64]{1,0:T(8,128)S(1)} %copy.38, pred[128,64]{1,0:T(8,128)(4,1)S(1)} %copy.37), kind=kLoop, calls=%fused_computation.2 | loop fusion | flops 32768 | bytes 172032 | tf_op jit(solution)/shard_map/jit(_where)/select_n | solution.py:66
  530.3 56.4 %scatter_custom_fusion = f32[2048,2]{1,0:T(8,128)S(1)} fusion(s32[8192]{0:T(1024)S(1)} %reshape.33, f32[8192,2]{1,0:T(8,128)} %bitcast.51, f32[]{:T(128)} %constant.8.clone.1), kind=kCustom, calls=%fused_computation.12 | custom fusion | flops 16384 | bytes 16896
  586.8 0.2 copy.39
  587.0 41.1 %all_gather.7 = bf16[512,2,128]{2,0,1:T(8,128)(2,1)S(1)} all-gather(bf16[16,2,128]{2,0,1:T(8,128)(2,1)S(1)} %bitcast.54), channel_id=1, replica_groups=mesh['row'=8,'col'=32] {'col'}, dimensions={0}, use_global_device_ids=true | all-gather | bytes 270336 | tf_op jit(solution)/shard_map/all_gather | solution.py:73
  628.2 0.3 convolution_bitcast_fusion
  628.5 0.3 convolution_bitcast_fusion.1
  628.8 0.1 fusion.11
  628.9 0.7 pad_maximum_fusion.3
  629.7 77.9 %reduce-scatter.2.cloned.1.call-done = bf16[512,2,16]{0,2,1:T(8,128)(2,1)} async-done(((bf16[512,2,128]{0,2,1:T(8,128)(2,1)}), bf16[512,2,16]{0,2,1:T(8,128)(2,1)}) %reduce-scatter.2.cloned.1.call-update) | async-done | bytes 32784 | tf_op jit(solution)/shard_map/reduce_scatter | solution.py:75
  707.5 0.8 convert_multiply_fusion
  708.3 1.4 broadcast_divide_fusion
  (33 shorter events, 0.6 us)
Async XLA Ops:
  7.2 51.2 %copy-start.5 = (s32[2]{0:T(128)S(1)}, s32[2]{0:T(128)}, u32[]{:S(2)}) copy-start(s32[2]{0:T(128)} %constant.34) | copy-start | bytes 28
  7.2 51.3 %copy-start.4 = (s32[2]{0:T(128)S(1)}, s32[2]{0:T(128)}, u32[]{:S(2)}) copy-start(s32[2]{0:T(128)} %constant.37) | copy-start | bytes 28
  7.2 51.1 %copy-start.1 = (s32[128,64]{0,1:T(8,128)S(1)}, s32[128,64]{0,1:T(8,128)}, u32[]{:S(2)}) copy-start(s32[128,64]{0,1:T(8,128)} %param.7) | copy-start | bytes 98308
  7.2 326.8 %all-reduce.3.cloned.1.call-start = ((), (), s32[]{:S(2)}) async-start(), calls=%async_computation.2 | async-start | bytes 1048576
  8.1 50.8 %copy-start.6 = (u32[256]{0:T(256)S(1)}, u32[256]{0:T(256)}, u32[]{:S(2)}) copy-start(u32[256]{0:T(256)} %constant.57) | copy-start | bytes 3076
  58.2 649.3 %reduce-scatter.2.cloned.1.call-start = ((), (), s32[]{:S(2)}) async-start(), calls=%async_computation.1 | async-start | bytes 294912 | tf_op jit(solution)/shard_map/reduce_scatter | solution.py:75
  432.5 89.2 %copy-start.2 = (s32[128,64]{0,1:T(8,128)S(1)}, s32[128,64]{0,1:T(8,128)}, u32[]{:S(2)}) copy-start(s32[128,64]{0,1:T(8,128)} %param.8) | copy-start | bytes 98308
  432.5 89.3 %copy-start.3 = (f32[128,64]{0,1:T(8,128)S(1)}, f32[128,64]{0,1:T(8,128)}, u32[]{:S(2)}) copy-start(f32[128,64]{0,1:T(8,128)} %param.9) | copy-start | bytes 98308
  522.6 105.6 %copy-start = (bf16[2,512,512]{2,1,0:T(8,128)(2,1)S(1)}, bf16[2,512,512]{2,1,0:T(8,128)(2,1)}, u32[]{:S(2)}) copy-start(bf16[2,512,512]{2,1,0:T(8,128)(2,1)} %param.5) | copy-start | bytes 3145732
Sparse Core Ops, SparseCore 0:
  58.4 275.5 all-reduce.2
  629.8 77.6 reduce-scatter.1
where the time goes:
time: 717 us
  waiting for transfers between devices  352 us (49%)
  blocking collectives  169 us (24%)
  local copies, waits for them, and re-layouts  107 us (15%)
  other arithmetic  70.4 us (10%)
  between operations  14.9 us (2%)
    unnamed x3, waiting for transfers between devices  274 us
    gather x1, local copies, waits for them, and re-layouts, trap_lookup(): values = block[clipped, :, pattern_ids]  88.8 us
    psum x1, blocking collectives, body(): amp = lax.psum(jnp.where(inside, amp_local, 0.0), ('row', 'col'))  81.6 us
    reduce_scatter x1, waiting for transfers between devices, body(): lax.psum_scatter(back.astype(jnp.bfloat16), 'row', scatter_dimension=2, t...  77.9 us
    unnamed x4, other arithmetic  56.5 us
    all_gather x1, blocking collectives, body(): whole = lax.all_gather(field, 'row', axis=2, tiled=True)  46.2 us
    all_gather x1, blocking collectives, body(): lax.all_gather(projected, 'col', axis=0, tiled=True)  41.1 us
  transfers between devices with their start and end apart: 2, of which 2 were waited for; matrix products, arithmetic and copies ran while one was open for 0% of the time, Pallas kernels for 0%

commit v1 on v0

--- a/solution.py
+++ b/solution.py
@@ -70,7 +70,13 @@
         .add(adds)
         .astype(jnp.bfloat16)
     )
-    total = back_terms(transfer, lax.all_gather(projected, "col", axis=0, tiled=True))
+    ends_arrange = lambda message, chip_axis: jnp.concatenate(
+        jax.lax.all_to_all(
+            jnp.stack([message for _ in range(jax.lax.axis_size(chip_axis))], 0), chip_axis, 0, 0
+        ),
+        0,
+    )
+    total = back_terms(transfer, ends_arrange(projected, "col"))
     back = total.reshape(modes_local, 2, count)
     back = lax.psum_scatter(
         back.astype(jnp.bfloat16), "row", scatter_dimension=2, tiled=True

time: 717 us -> 692 us (0.965)
  blocking collectives: 169 us -> 143 us
    all_gather x1 -> x0, blocking collectives: 41.1 us -> none  [body(): lax.all_gather(projected, 'col', axis=0, tiled=True)]
    all_to_all x0 -> x1, blocking collectives: none -> 15 us  [body(): jax.lax.all_to_all(jnp.stack([message for _ in range(jax.lax.axis_size(ch...]
where the time goes in v1:
time: 692 us
  waiting for transfers between devices  353 us (51%)
  blocking collectives  143 us (21%)
  local copies, waits for them, and re-layouts  107 us (15%)
  other arithmetic  70.4 us (10%)
  between operations  14.9 us (2%)
    unnamed x3, waiting for transfers between devices  274 us
    gather x1, local copies, waits for them, and re-layouts, trap_lookup(): values = block[clipped, :, pattern_ids]  88.8 us
    psum x1, blocking collectives, body(): amp = lax.psum(jnp.where(inside, amp_local, 0.0), ('row', 'col'))  81.6 us
    reduce_scatter x1, waiting for transfers between devices, body(): lax.psum_scatter(back.astype(jnp.bfloat16), 'row', scatter_dimension=2, t...  79 us
    unnamed x4, other arithmetic  56.6 us
    all_gather x1, blocking collectives, body(): whole = lax.all_gather(field, 'row', axis=2, tiled=True)  46.2 us
    all_to_all x1, blocking collectives, body(): jax.lax.all_to_all(jnp.stack([message for _ in range(jax.lax.axis_size(ch...  15 us
  transfers between devices with their start and end apart: 2, of which 2 were waited for; matrix products, arithmetic and copies ran while one was open for 0% of the time, Pallas kernels for 0%

profile of v1, /device:TPU:2, one launch (start us, length us, event | category | flops | bytes accessed | tf_op | source)
XLA Modules:
  0.0 691.6 jit_solution(10233618889842682017)
XLA Ops:
  7.2 0.9 fusion.20
  8.2 46.2 %all_gather.3 = bf16[2,512,128]{1,2,0:T(8,128)(2,1)S(1)} all-gather(bf16[2,512,16]{1,2,0:T(8,128)(2,1)S(1)} %pad_maximum_fusion.8), channel_id=1, replica_groups=mesh['row'=8,'col'=32] {'row'}, dimensions={2}, use_global_device_ids=true | all-gather | bytes 294912 | tf_op jit(solution)/shard_map/all_gather | solution.py:41
  54.3 1.4 convolution_bitcast_fusion.2
  55.7 1.4 convolution_bitcast_fusion.3
  57.1 0.1 fusion.13
  57.2 1.0 copy.31
  58.4 0.1 and_reduce_fusion
  58.5 0.1 copy.36
  58.7 0.1 copy.32
  58.9 0.6 dynamic-slice
  60.1 273.9 %all-reduce.3.cloned.1.call-done = f32[512,2,128]{2,1,0:T(2,128)} async-done(((f32[512,2,128]{2,1,0:T(2,128)}), f32[512,2,128]{2,1,0:T(2,128)}) %all-reduce.3.cloned.1.call-update) | async-done | bytes 524304
  334.0 1.3 fusion.27
  335.3 0.4 copy.33
  335.7 88.8 %gather_fusion = f32[8192,2]{1,0:T(8,128)} fusion(f32[16,2,128]{1,2,0:T(8,128)S(1)} %copy.33, s32[8192]{0:T(1024)S(1)} %reshape.33), kind=kCustom, calls=%fused_computation | custom fusion | bytes 196608 | tf_op jit(solution)/shard_map/gather | solution.py:31
  424.5 8.0 %fusion.28 = (f32[128,64,1]{2,1,0:T(8,128)}, f32[128,64,1]{2,1,0:T(8,128)}) fusion(f32[128,64,2]{2,1,0:T(8,128)} %bitcast.51), kind=kLoop, calls=%fused_computation.66 | loop fusion | bytes 131072 | tf_op jit(solution)/shard_map/slice | solution.py:61
  432.5 3.8 copy.41
  436.3 3.7 copy.42
  440.0 81.6 %psum.7 = f32[128,64]{0,1:T(8,128)S(1)} all-reduce(f32[128,64]{0,1:T(8,128)S(1)} %get-tuple-element.14), channel_id=1, replica_groups=mesh['row'=8,'col'=32] {'row','col'}, use_global_device_ids=true, to_apply=%region_1.2 | all-reduce | flops 8192 | bytes 65536 | tf_op jit(solution)/shard_map/psum | solution.py:62
  521.7 0.1 copy.37
  521.8 0.6 multiply_divide_fusion
  522.5 0.1 copy.38
  522.6 7.7 %multiply_select_fusion = f32[128,64,2]{2,1,0:T(8,128)} fusion(f32[128,64,2]{2,1,0:T(8,128)} %bitcast.52, f32[128,64]{1,0:T(8,128)S(1)} %copy.38, pred[128,64]{1,0:T(8,128)(4,1)S(1)} %copy.37), kind=kLoop, calls=%fused_computation.2 | loop fusion | flops 32768 | bytes 172032 | tf_op jit(solution)/shard_map/jit(_where)/select_n | solution.py:66
  530.2 56.4 %scatter_custom_fusion = f32[2048,2]{1,0:T(8,128)S(1)} fusion(s32[8192]{0:T(1024)S(1)} %reshape.39, f32[8192,2]{1,0:T(8,128)} %bitcast.53, f32[]{:T(128)} %constant.8.clone.1), kind=kCustom, calls=%fused_computation.12 | custom fusion | flops 16384 | bytes 16896
  586.7 0.2 copy.39
  587.0 15.0 %all_to_all.5 = bf16[32,16,2,128]{3,1,2,0:T(8,128)(2,1)S(1)} all-to-all(bf16[32,16,2,128]{3,1,2,0:T(8,128)(2,1)S(1)} %stack.23), channel_id=1, replica_groups=mesh['row'=8,'col'=32] {'col'}, dimensions={0} | all-to-all | bytes 524288 | tf_op jit(solution)/shard_map/all_to_all | solution.py:74
  602.1 0.3 convolution_bitcast_fusion
  602.4 0.3 convolution_bitcast_fusion.1
  602.8 0.1 fusion.11
  602.9 0.7 pad_maximum_fusion.3
  603.6 79.0 %reduce-scatter.2.cloned.1.call-done = bf16[512,2,16]{0,2,1:T(8,128)(2,1)} async-done(((bf16[512,2,128]{0,2,1:T(8,128)(2,1)}), bf16[512,2,16]{0,2,1:T(8,128)(2,1)}) %reduce-scatter.2.cloned.1.call-update) | async-done | bytes 32784 | tf_op jit(solution)/shard_map/reduce_scatter | solution.py:81
  682.6 0.8 convert_multiply_fusion
  683.4 1.4 broadcast_divide_fusion
  (35 shorter events, 0.7 us)
Async XLA Ops:
  7.2 51.2 %copy-start.5 = (s32[2]{0:T(128)S(1)}, s32[2]{0:T(128)}, u32[]{:S(2)}) copy-start(s32[2]{0:T(128)} %constant.34) | copy-start | bytes 28
  7.2 51.3 %copy-start.4 = (s32[2]{0:T(128)S(1)}, s32[2]{0:T(128)}, u32[]{:S(2)}) copy-start(s32[2]{0:T(128)} %constant.37) | copy-start | bytes 28
  7.2 51.1 %copy-start.1 = (s32[128,64]{0,1:T(8,128)S(1)}, s32[128,64]{0,1:T(8,128)}, u32[]{:S(2)}) copy-start(s32[128,64]{0,1:T(8,128)} %param.7) | copy-start | bytes 98308
  7.2 326.8 %all-reduce.3.cloned.1.call-start = ((), (), s32[]{:S(2)}) async-start(), calls=%async_computation.3 | async-start | bytes 1048576
  8.1 50.8 %copy-start.6 = (u32[256]{0:T(256)S(1)}, u32[256]{0:T(256)}, u32[]{:S(2)}) copy-start(u32[256]{0:T(256)} %constant.57) | copy-start | bytes 3076
  58.2 624.4 %reduce-scatter.2.cloned.1.call-start = ((), (), s32[]{:S(2)}) async-start(), calls=%async_computation.2 | async-start | bytes 294912 | tf_op jit(solution)/shard_map/reduce_scatter | solution.py:81
  432.5 89.2 %copy-start.2 = (s32[128,64]{0,1:T(8,128)S(1)}, s32[128,64]{0,1:T(8,128)}, u32[]{:S(2)}) copy-start(s32[128,64]{0,1:T(8,128)} %param.8) | copy-start | bytes 98308
  432.5 89.3 %copy-start.3 = (f32[128,64]{0,1:T(8,128)S(1)}, f32[128,64]{0,1:T(8,128)}, u32[]{:S(2)}) copy-start(f32[128,64]{0,1:T(8,128)} %param.9) | copy-start | bytes 98308
  530.2 71.9 %copy-start = (bf16[2,512,512]{2,1,0:T(8,128)(2,1)S(1)}, bf16[2,512,512]{2,1,0:T(8,128)(2,1)}, u32[]{:S(2)}) copy-start(bf16[2,512,512]{2,1,0:T(8,128)(2,1)} %param.5) | copy-start | bytes 3145732
Sparse Core Ops, SparseCore 0:
  58.4 275.5 all-reduce.2
  603.7 78.8 reduce-scatter.1
